TPU v7x, 256 devices: a whole 4x4x8 slice. The times are simulated.
256 devices in a mesh: tm: 16 (over y, z_hi), chan: 16 (over z_lo, x, core).
Axes of the slice: x: 4, y: 4, z: 8 (z_hi: 4, z_lo: 2; z = z_hi * 2 + z_lo), core: 2. Of those that a mesh axis runs over, the one named last changes fastest.
Arguments:
- raw_strain: bfloat16 [4096, 81920], P('chan', 'tm'), may hold values from -48 to 48
- fir_taps: float32 [128], replicated, may hold values from -0.5 to 0.5
- source_channels: int32 [256], replicated, may hold values from 0 to 4095, as said below
- live_counts: int32 [256], P(('chan', 'tm')), may hold values from 8 to 16, as said below
Outputs:
- correlations: float32 [256, 4096, 384], P(None, ('chan', 'tm'))
Inputs may be any that keep to these rules, and one draw needn't show every extreme that they name: `source_channels`: the virtual sources are distinct live channels; at most 2 of them lie in one aligned block of 16 channels, and some block holds exactly 2. `live_counts`: some block has all 16 channels live and some has exactly half of them.
All inputs are finite; a program needn't handle non-finite values.
Results may differ from a plain program's by a relative error of at most 0.015.
Values may be sent and summed in bfloat16 or wider, within the bound.
A program may use at most 128 MiB of HBM per device.

v0:
```python
import functools
import math

import jax
import jax.numpy as jnp
import numpy as np
from jax import lax
from jax.experimental import pallas as pl
from jax.experimental.pallas import tpu as pltpu
from jax.sharding import PartitionSpec as P

NX, NY, NZ, NC = 4, 4, 8, 2
TM, CHAN = 16, 16
DECIM, SEG, BAND, LAGH = 10, 1024, 64, 192
NSEG = 8
HALF = SEG // 2
SRC = 256
SLOTS = 512
EPS = 1e-06
MESH = pl.DeviceIdType.MESH
F32, BF16 = jnp.float32, jnp.bfloat16
TAPS = 128
REACH = 1408
KG = HALF // BAND
PARTS = ((0, 2), (2, 3), (5, 3))


def dot(a, b):
    return jnp.dot(a, b, preferred_element_type=F32)


def hi_lo(table):
    hi = table.astype(np.float32).astype(jnp.bfloat16)
    lo = (table - hi.astype(np.float64)).astype(np.float32).astype(jnp.bfloat16)
    return hi, lo


def dft_table():
    n = np.arange(HALF)[:, None]
    k = np.arange(HALF)[None, :]
    phase = (n * k % SEG) * (2.0 * np.pi / SEG)
    both = np.stack([np.cos(phase), -np.sin(phase)], axis=1).reshape(HALF, 2, KG, BAND)
    table = both.transpose(0, 2, 1, 3).reshape(HALF, SEG)
    return np.concatenate(hi_lo(table), axis=1)


def lag_table():
    k = np.arange(HALF)[:, None]
    t = np.arange(-LAGH, LAGH)[None, :]
    phase = (k * t % SEG) * (2.0 * np.pi / SEG)
    weight = np.where(k == 0, 1.0, 2.0) * (math.sqrt(SEG / NSEG) / SEG)
    both = np.stack([weight * np.cos(phase), -weight * np.sin(phase)], axis=0)
    table = both.reshape(2, KG, BAND, 2 * LAGH).transpose(1, 0, 2, 3).reshape(SEG, 2 * LAGH)
    return table.astype(np.float32).astype(jnp.bfloat16)


def whiten(spec):
    bands = []
    for band in range(KG):
        block = spec[:, band * 128 : (band + 1) * 128]
        power = jnp.sum(block * block, axis=1, keepdims=True) * (1.0 / BAND)
        bands.append(block * lax.rsqrt(power + EPS))
    return jnp.concatenate(bands, axis=1).astype(BF16)


def odd_sign(rows):
    lane = lax.broadcasted_iota(jnp.int32, (rows, SEG), 1)
    return (1 - 2 * lax.rem(lane, 2)).astype(F32)


def place(x, y, z, core):
    return (y * 4 + z // 2, lax.rem(z, 2) * 8 + x * 2 + core)


def gather_part(buf, semaphores, core, order, step_dir, sends, first):
    send_sem, recv_sem = semaphores
    count = 0
    for stage, (me, size, chunk, device) in enumerate(order):
        far, near = size // 2, size - 1 - size // 2

        def index(offset):
            return lax.rem(me + step_dir * offset + size, size)

        def send(src, dst, to, number):
            copy = pltpu.make_async_remote_copy(
                src_ref=src,
                dst_ref=dst,
                send_sem=send_sem.at[number],
                recv_sem=recv_sem.at[number],
                device_id=device(index(to)),
                device_id_type=MESH,
            )
            copy.start()
            sends.append(copy)

        def arrived(offset, number):
            block = chunk(index(offset))
            pltpu.make_async_remote_copy(
                src_ref=block,
                dst_ref=block,
                send_sem=send_sem.at[number],
                recv_sem=recv_sem.at[number],
                device_id=device(index(1)),
                device_id_type=MESH,
            ).wait_recv()
            return block

        own = chunk(me)
        start = first if stage == 0 else own
        send(start, own, 1, count)
        send(start, own, -1, count + far)
        last = stage == len(order) - 1
        if last:
            yield own
        for hop in range(1, far + 1):
            yield None
            block = arrived(-hop, count + hop - 1)
            if hop < far:
                send(block, block, 1, count + hop)
            if last:
                yield block
            if hop <= near:
                block = arrived(hop, count + far + hop - 1)
                if hop < near:
                    send(block, block, -1, count + far + hop)
                if last:
                    yield block
        count += far + near


def gather_kernel(
    raw_hbm, rev_ref, src_ref, live_ref, table_hbm,
    a_ref, b_ref, c_ref, white_ref,
    raw_v, tap_v, dec_v, sel_v, pair_v, trace_v, table_v, own_v,
    load_sem, table_sem, halo_sem, pair_sem, trace_send, trace_recv,
    a_send, a_recv, b_send, b_recv, c_send, c_recv, own_sem, twin_send, twin_recv,
):
    tm = lax.axis_index("tm")
    chan = lax.axis_index("chan")
    y, z_hi = tm // 4, lax.rem(tm, 4)
    z_lo, x, core = chan // 8, lax.rem(chan, 8) // 2, lax.rem(chan, 2)
    z = z_hi * 2 + z_lo
    direction = 1 - 2 * core
    half = lax.rem(tm, 2)

    def remote(src, dst, sems, device):
        return pltpu.make_async_remote_copy(
            src_ref=src, dst_ref=dst, send_sem=sems[0], recv_sem=sems[1], device_id=device, device_id_type=MESH
        )

    loads = []
    for part in range(4):
        loads.append(
            pltpu.make_async_copy(
                raw_hbm.at[:, part * 1280 : (part + 1) * 1280],
                raw_v.at[:, 128 + part * 1280 : 128 + (part + 1) * 1280],
                load_sem.at[part],
            )
        )
        loads[-1].start()
    table_load = pltpu.make_async_copy(table_hbm, table_v, table_sem)
    table_load.start()

    barrier = pltpu.get_barrier_semaphore()
    peers = [(lax.rem(tm + step, TM), chan) for step in range(1, TM)]
    for to_x in (1, 3):
        peers.append(place(lax.rem(x + to_x, NX), y, z, core))
    for to_z in (1, 7):
        peers.append(place(x, y, lax.rem(z + to_z, NZ), core))
    twin = place(x, y, z, 1 - core)
    peers.append(twin)
    for peer in peers:
        pl.semaphore_signal(barrier, inc=1, device_id=peer, device_id_type=MESH)
    pl.semaphore_wait(barrier, len(peers))

    halo = remote(
        raw_hbm.at[:, 4992:5120], raw_v.at[:, 0:128], (halo_sem.at[0], halo_sem.at[1]), (lax.rem(tm + 1, TM), chan)
    )
    halo.start()

    base = pltpu.roll(jnp.broadcast_to(rev_ref[...], (8, 384)), 0, 1, stride=DECIM, stride_axis=0)
    for group in range(8):
        rows = []
        for octet in (2 * group, 2 * group + 1):
            at, turn = divmod(octet * 8 * DECIM, 128)
            piece = pltpu.roll(base, turn, 1) if turn else base
            blocks = [jnp.zeros((8, 128), F32)] * (REACH // 128)
            for number in range(min(3, REACH // 128 - at)):
                blocks[at + number] = piece[:, number * 128 : (number + 1) * 128]
            rows.append(jnp.concatenate(blocks, axis=1))
        band = jnp.concatenate(rows, axis=0)
        band_hi = band.astype(BF16)
        tap_v[group * 16 : group * 16 + 16, :] = band_hi
        tap_v[128 + group * 16 : 128 + group * 16 + 16, :] = (band - band_hi.astype(F32)).astype(BF16)

    src = src_ref[...].astype(F32)
    src_col = jnp.transpose(jnp.broadcast_to(src, (SRC, SRC)))
    lane = lax.broadcasted_iota(jnp.int32, (SRC, SRC), 1)
    row = lax.broadcasted_iota(jnp.int32, (SRC, SRC), 0)
    hit = jnp.where(src_col == (lane + chan * 256).astype(F32), 1.0, 0.0)
    is_src = jnp.sum(hit, axis=0, keepdims=True)
    earlier = jnp.where((row // 16 == lane // 16) & (row < lane), 1.0, 0.0)
    rank = dot(jnp.broadcast_to(is_src, (16, SRC)).astype(BF16), earlier.astype(BF16))[0:1, :]
    pick_row = lax.broadcasted_iota(jnp.int32, (32, SRC), 0)
    pick_lane = lax.broadcasted_iota(jnp.int32, (32, SRC), 1)
    pick = jnp.where(
        (pick_row // 2 == pick_lane // 16) & (lax.rem(pick_row, 2).astype(F32) == rank) & (is_src > 0.5), 1.0, 0.0
    ).astype(BF16)

    for part in (1, 2, 3, 0):
        if part == 1:
            loads[0].wait()
        if part:
            loads[part].wait()
        else:
            halo.wait()

            @pl.when(tm == 0)
            def _():
                raw_v[:, 0:128] = jnp.zeros((256, 128), BF16)

        both = lax.dot_general(
            raw_v[:, part * 1280 : part * 1280 + REACH],
            tap_v[...],
            (((1,), (1,)), ((), ())),
            preferred_element_type=F32,
        )
        dec_v[:, part * 128 : (part + 1) * 128] = (both[:, 0:128] + both[:, 128:256]).astype(BF16)

    picked = dot(pick, dec_v[...]).astype(BF16)
    sel_v[0] = picked[0:16]
    sel_v[1] = picked[16:32]
    pair = remote(
        sel_v.at[1 - half], pair_v, (pair_sem.at[0], pair_sem.at[1]), (tm + 1 - 2 * half, chan)
    )
    pair.start()

    traces = []
    for step in range(1, TM):
        to = lax.rem(tm + step, TM)
        copy = remote(
            dec_v.at[pl.ds(pl.multiple_of(to * 16, 16), 16), :],
            trace_v.at[tm],
            (trace_send.at[step - 1], trace_recv.at[step - 1]),
            (to, chan),
        )
        copy.start()
        traces.append(copy)
    trace_v[tm] = dec_v[pl.ds(pl.multiple_of(tm * 16, 16), 16), :]

    table_load.wait()
    pair.wait()
    spec = dot(jnp.concatenate([sel_v[half], pair_v[...]], axis=0), table_v[...])
    mine = spec[0:16, 0:SEG] + spec[0:16, SEG:]
    other = spec[16:32, 0:SEG] + spec[16:32, SEG:]
    is_first = half == 0
    sign = odd_sign(16)
    own_v[...] = whiten(jnp.where(is_first, mine, other) + sign * jnp.where(is_first, other, mine))

    def part_order(buf, axes):
        sizes = {"x": NX, "y": NY, "z": NZ}
        at = {"x": x, "y": y, "z": z}
        order = []
        for number, axis in enumerate(axes):
            lead = [at[a] for a in reversed(axes[number + 1 :])]

            def chunk(index, lead=lead):
                return buf.at[(core, *lead, index)]

            def device(index, axis=axis):
                where = dict(at)
                where[axis] = index
                return place(where["x"], where["y"], where["z"], core)

            order.append((at[axis], sizes[axis], chunk, device))
        return order

    sends = []
    routines = []
    own_copies = []
    bufs = ((a_ref, "xyz", a_send, a_recv), (b_ref, "yzx", b_send, b_recv), (c_ref, "zxy", c_send, c_recv))
    for number, (buf, axes, send_sem, recv_sem) in enumerate(bufs):
        begin, bands = PARTS[number]
        first = own_v.at[:, begin * 128 : (begin + bands) * 128]
        at = {"x": x, "y": y, "z": z}
        slot = buf.at[(core, *(at[a] for a in reversed(axes)))]
        copy = pltpu.make_async_copy(first, slot, own_sem.at[number])
        copy.start()
        own_copies.append(copy)
        order = part_order(buf, axes)
        routines.append(gather_part(buf, (send_sem, recv_sem), core, order, direction, sends, first))

    twins = []

    def to_twin(block):
        number = len(twins)
        copy = remote(block, block, (twin_send.at[number], twin_recv.at[number]), twin)
        copy.start()
        twins.append(copy)

    live = list(routines)
    round_number = 0
    while live:
        for routine in list(live):
            while True:
                try:
                    block = next(routine)
                except StopIteration:
                    live.remove(routine)
                    break
                if block is None:
                    break
                to_twin(block)
        if round_number == 0:
            for copy in own_copies:
                copy.wait()
            for copy in traces:
                copy.wait()
            rows = lax.broadcasted_iota(jnp.int32, (256, HALF), 0)
            alive = lax.rem(rows, 16) < live_ref[0]
            flat = trace_v[...].reshape(256, HALF)
            spec = dot(jnp.where(alive, flat, jnp.zeros_like(flat)), table_v[...])
            for seg in range(NSEG):
                low = spec[seg * 32 : seg * 32 + 16]
                high = spec[seg * 32 + 16 : seg * 32 + 32]
                full = low[:, 0:SEG] + low[:, SEG:] + sign * (high[:, 0:SEG] + high[:, SEG:])
                white = whiten(full).astype(F32)
                for band in range(KG):
                    white_ref[band, pl.ds(seg, 16, stride=NSEG), :] = white[:, band * 128 : (band + 1) * 128]
        round_number += 1
    for copy in sends:
        copy.wait_send()
    for copy in twins:
        copy.wait()


def correlate_kernel(src_ref, white_ref, a_ref, b_ref, c_ref, lag_ref, out_hbm, all_v, weight_v, cross_v, out_v, out_sem):
    src = src_ref[...].astype(F32)
    src_row = jnp.broadcast_to(src, (SRC, SRC))
    src_col = jnp.transpose(src_row)
    row_block = jnp.floor(src_row * (1.0 / 16))
    col_block = jnp.floor(src_col * (1.0 / 16))
    before = jnp.where((row_block == col_block) & (src_row < src_col), 1.0, 0.0)
    rank = jnp.sum(before, axis=1, keepdims=True).astype(jnp.int32)
    block = col_block[:, 0:1].astype(jnp.int32)
    chan = block // 16
    local = lax.rem(block, 16)
    run = (local // 8) * 2 + chan // 8
    slot = 2 * lax.rem(local, 8) + rank
    where = run * 128 + lax.rem(chan, 8) * 16 + slot
    pick = jnp.where(where == lax.broadcasted_iota(jnp.int32, (SRC, SLOTS), 1), 1.0, 0.0).astype(BF16)
    for seg in range(NSEG):
        y, run0 = seg // 2, (seg % 2) * 4
        at = [(x, y, z, core) for z in range(run0, run0 + 4) for x in range(NX) for core in range(NC)]
        pieces = (
            [a_ref[core, z, y, x] for x, y, z, core in at],
            [b_ref[core, x, z, y] for x, y, z, core in at],
            [c_ref[core, y, x, z] for x, y, z, core in at],
        )
        for number, (begin, bands) in enumerate(PARTS):
            rows = dot(pick, jnp.concatenate(pieces[number], axis=0)).astype(BF16)
            for band in range(bands):
                lane = ((begin + band) * NSEG + seg) * 128
                all_v[:, lane : lane + 128] = rows[:, band * 128 : (band + 1) * 128]

    half = BAND
    row = lax.broadcasted_iota(jnp.int32, (half, 128), 0)
    lane = lax.broadcasted_iota(jnp.int32, (half, 128), 1)
    same = row == lax.rem(lane, half)
    sign = jnp.where(lane[0:1] < half, 1.0, -1.0)

    def copies(which):
        return [
            pltpu.make_async_copy(
                out_v.at[which, part].reshape(SRC, 8, 128),
                out_hbm.at[:, which * 8 : which * 8 + 8, part * 128 : (part + 1) * 128],
                out_sem.at[which, part],
            )
            for part in range(3)
        ]

    @pl.loop(0, 8)
    def _(pair):
        for band in range(KG):
            for seg in range(NSEG):
                for which in range(2):
                    v = white_ref[band, 2 * pair + which, seg : seg + 1, :]
                    u = sign * pltpu.roll(v, half, 1)
                    lanes = slice(which * 128, which * 128 + 128)
                    weight_v[band % 2, seg * 128 : seg * 128 + half, lanes] = jnp.where(same, v, 0.0).astype(BF16)
                    weight_v[band % 2, seg * 128 + half : seg * 128 + 128, lanes] = jnp.where(same, u, 0.0).astype(BF16)
            cross = dot(all_v[:, band * 1024 : (band + 1) * 1024], weight_v[band % 2]).astype(BF16)
            for which in range(2):
                cross_v[which, :, band * 128 : (band + 1) * 128] = cross[:, which * 128 : (which + 1) * 128]
        for which in range(2):
            lags = dot(cross_v[which], lag_ref[...])
            spot = lax.rem(pair, 4) * 2 + which
            for part in range(3):
                out_v[pair // 4, part, pl.ds(spot, SRC, stride=8), :] = lags[:, part * 128 : (part + 1) * 128]
        for which in range(2):

            @pl.when(pair == which * 4 + 3)
            def _():
                for copy in copies(which):
                    copy.start()

    for which in range(2):
        for copy in copies(which):
            copy.wait()


def local(raw_strain, fir_taps, source_channels, live_counts):
    rev = jnp.pad(jnp.flip(fir_taps), (1, 384 - 1 - TAPS))[None, :]
    src = source_channels[None, :]
    any_spec = pl.BlockSpec(memory_space=pl.ANY)
    vmem = pl.BlockSpec(memory_space=pltpu.VMEM)
    dma = pltpu.SemaphoreType.DMA
    widths = [bands * 128 for _, bands in PARTS]
    hops = NX - 1 + NY - 1 + NZ - 1
    blocks = NX + NY + NZ
    a, b, c, white = pl.pallas_call(
        gather_kernel,
        out_shape=(
            jax.ShapeDtypeStruct((NC, NZ, NY, NX, 16, widths[0]), BF16),
            jax.ShapeDtypeStruct((NC, NX, NZ, NY, 16, widths[1]), BF16),
            jax.ShapeDtypeStruct((NC, NY, NX, NZ, 16, widths[2]), BF16),
            jax.ShapeDtypeStruct((KG, 16 * NSEG, 128), F32),
        ),
        in_specs=[any_spec, vmem, vmem, pl.BlockSpec(memory_space=pltpu.SMEM), any_spec],
        out_specs=(vmem, vmem, vmem, vmem),
        scratch_shapes=[
            pltpu.VMEM((256, 5248), BF16),
            pltpu.VMEM((256, REACH), BF16),
            pltpu.VMEM((256, HALF), BF16),
            pltpu.VMEM((2, 16, HALF), BF16),
            pltpu.VMEM((16, HALF), BF16),
            pltpu.VMEM((TM, 16, HALF), BF16),
            pltpu.VMEM((HALF, 2 * SEG), BF16),
            pltpu.VMEM((16, SEG), BF16),
            dma((4,)),
            dma,
            dma((2,)),
            dma((2,)),
            dma((TM - 1,)),
            dma((TM - 1,)),
            dma((hops,)),
            dma((hops,)),
            dma((hops,)),
            dma((hops,)),
            dma((hops,)),
            dma((hops,)),
            dma((3,)),
            dma((blocks,)),
            dma((blocks,)),
        ],
        compiler_params=pltpu.CompilerParams(
            collective_id=0, has_side_effects=True, vmem_limit_bytes=60 * 1024 * 1024
        ),
        name="filter_and_gather",
    )(raw_strain, rev, src, live_counts, jnp.asarray(dft_table()))
    return pl.pallas_call(
        correlate_kernel,
        out_shape=jax.ShapeDtypeStruct((SRC, 16, 2 * LAGH), F32),
        in_specs=[vmem, vmem, vmem, vmem, vmem, vmem],
        out_specs=any_spec,
        scratch_shapes=[
            pltpu.VMEM((SRC, NSEG * SEG), BF16),
            pltpu.VMEM((2, SEG, 256), BF16),
            pltpu.VMEM((2, SRC, SEG), BF16),
            pltpu.VMEM((2, 3, SRC * 8, 128), F32),
            dma((2, 3)),
        ],
        compiler_params=pltpu.CompilerParams(vmem_limit_bytes=60 * 1024 * 1024),
        name="correlate",
    )(src, white.reshape(KG, 16, NSEG, 128), a, b, c, jnp.asarray(lag_table()))


def solution(mesh):
    placed = (P("chan", "tm"), P(), P(), P(("chan", "tm")))
    return jax.shard_map(
        local, mesh=mesh, in_specs=placed, out_specs=P(None, ("chan", "tm"), None), check_vma=False
    )
```

profile of v0, /device:TPU:1, one launch (start us, length us, event | category | flops | bytes accessed | tf_op | source)
XLA Modules:
  0.0 96.3 jit_solution(6835144299988469795)
XLA Ops:
  0.7 0.7 rev.4
  1.4 0.1 pad.4
  1.5 0.6 broadcast_in_dim.7.rev_ref
  2.0 68.6 %filter_and_gather.1 = (bf16[2,8,4,4,16,256]{5,4,3,2,1,0:T(8,128)(2,1)}, bf16[2,4,8,4,16,384]{5,4,3,2,1,0:T(8,128)(2,1)}, bf16[2,4,4,8,16,384]{5,4,3,2,1,0:T(8,128)(2,1)}, f32[8,128,128]{2,1,0:T(8,128)}) custom-call(bf16[256,5120]{1,0:T(8,128)(2,1)} %raw_hbm.1, f32[1,384]{1,0:T(1,128)} %broadcast_in_dim.7.rev_ref, s32[1,256]{1,0:T(1,128)} %bitcast.3, ...), custom_call_target="tpu_custom_call" | custom-call | tf_op jit(solution)/shard_map/filter_and_gather/pallas_call | solution.py:421
  70.6 25.7 %correlate.1 = f32[256,16,384]{2,1,0:T(8,128)} custom-call(s32[1,256]{1,0:T(1,128)} %bitcast.4, f32[8,16,8,128]{3,2,1,0:T(8,128)} %bitcast.2, bf16[2,8,4,4,16,256]{5,4,3,2,1,0:T(8,128)(2,1)} %get-tuple-element.10.a_ref, bf16[2,4,8,4,16,384]{5,4,3,2,1,0:T(8,128)(2,1)} %get-tuple-element.11.b_ref, bf16[2,4,4,8,16,384]{5,4,3,2,1,0:T(8,128)(2,1)} %get-tuple-element.12.c_ref, ...), custom_call_target="tpu_custom_call" | custom-call | tf_op jit(solution)/shard_map/correlate/pallas_call | solution.py:461
where the time goes:
time: 97.6 us; the launch traced here: 96.3 us
  Pallas kernels  94.3 us (97%)
  local copies, waits for them, and re-layouts  1.39 us (1%)
    pallas_call x1, Pallas kernels, local(): pl.pallas_call(gather_kernel, out_shape=(jax.ShapeDtypeStruct((NC, NZ, NY...  68.6 us
    pallas_call x1, Pallas kernels, local(): pl.pallas_call(correlate_kernel, out_shape=jax.ShapeDtypeStruct((SRC, 16,...  25.7 us

commit v1 on v0

v1 whole, which is shorter than its diff:
```python
import functools
import math

import jax
import jax.numpy as jnp
import numpy as np
from jax import lax
from jax.experimental import pallas as pl
from jax.experimental.pallas import tpu as pltpu
from jax.sharding import PartitionSpec as P

NX, NY, NZ, NC = 4, 4, 8, 2
TM, CHAN = 16, 16
DECIM, SEG, BAND, LAGH = 10, 1024, 64, 192
NSEG = 8
HALF = SEG // 2
SRC = 256
SLOTS = 512
EPS = 1e-06
MESH = pl.DeviceIdType.MESH
F32, BF16 = jnp.float32, jnp.bfloat16
TAPS = 128
REACH = 1408
KG = HALF // BAND
QUARTERS, BINS = 4, 16
QUOTA = SRC // NX
PARTS = ((0, 16), (16, 16), (32, 32))
ROUNDS = "ABCABACABABCAC"


def dot(a, b):
    return jnp.dot(a, b, preferred_element_type=F32)


def hi_lo(table):
    hi = table.astype(np.float32).astype(jnp.bfloat16)
    lo = (table - hi.astype(np.float64)).astype(np.float32).astype(jnp.bfloat16)
    return hi, lo


def dft_table():
    n = np.arange(HALF)[:, None]
    k = np.arange(HALF)[None, :]
    phase = (n * k % SEG) * (2.0 * np.pi / SEG)
    both = np.stack([np.cos(phase), -np.sin(phase)], axis=1).reshape(HALF, 2, KG, QUARTERS, BINS)
    table = both.transpose(0, 2, 3, 1, 4).reshape(HALF, SEG)
    return np.concatenate(hi_lo(table), axis=1)


def lag_table():
    k = np.arange(HALF)[:, None]
    t = np.arange(-LAGH, LAGH)[None, :]
    phase = (k * t % SEG) * (2.0 * np.pi / SEG)
    weight = np.where(k == 0, 1.0, 2.0) * (math.sqrt(SEG / NSEG) / SEG)
    both = np.stack([weight * np.cos(phase), -weight * np.sin(phase)], axis=0)
    table = both.reshape(2, KG, QUARTERS, BINS, 2 * LAGH).transpose(1, 2, 0, 3, 4).reshape(SEG, 2 * LAGH)
    return table.astype(np.float32).astype(jnp.bfloat16)


def whiten(spec, turn=None):
    bands = []
    for band in range(KG):
        block = spec[:, band * 128 : (band + 1) * 128]
        power = jnp.sum(block * block, axis=1, keepdims=True) * (1.0 / BAND)
        block = block * lax.rsqrt(power + EPS)
        bands.append(block if turn is None else pltpu.roll(block, turn, 1))
    return jnp.concatenate(bands, axis=1).astype(BF16)


def odd_sign(rows):
    lane = lax.broadcasted_iota(jnp.int32, (rows, SEG), 1)
    return (1 - 2 * lax.rem(lane, 2)).astype(F32)


def place(x, y, z, core):
    return (y * 4 + z // 2, lax.rem(z, 2) * 8 + x * 2 + core)


def gather_part(semaphores, order, step_dir, sends, first):
    send_sem, recv_sem = semaphores
    count = 0
    for stage, (me, size, chunk, device) in enumerate(order):

        def index(offset):
            return lax.rem(me + step_dir * offset + size, size)

        def copy_of(src, to, number):
            return pltpu.make_async_remote_copy(
                src_ref=src[0],
                dst_ref=src[1],
                send_sem=send_sem.at[number],
                recv_sem=recv_sem.at[number],
                device_id=device(index(to)),
                device_id_type=MESH,
            )

        def send(src, dst, to, number):
            copy = copy_of((src, dst), to, number)
            copy.start()
            sends.append(copy)

        def arrived(offset, number):
            block = chunk(index(offset))
            copy_of((block, block), 1, number).wait_recv()
            return block

        own = chunk(me)
        start = first if stage == 0 else own
        if stage < len(order) - 1:
            for offset in range(1, size):
                send(start, own, offset, count + offset - 1)
            yield None
            for offset in range(1, size):
                arrived(-offset, count + offset - 1)
            count += size - 1
            continue
        far, near = size // 2, size - 1 - size // 2
        send(own, own, 1, count)
        send(own, own, -1, count + far)
        yield own
        for hop in range(1, far + 1):
            yield None
            block = arrived(-hop, count + hop - 1)
            if hop < far:
                send(block, block, 1, count + hop)
            yield block
            if hop <= near:
                block = arrived(hop, count + far + hop - 1)
                if hop < near:
                    send(block, block, -1, count + far + hop)
                yield block


def gather_kernel(
    raw_hbm, rev_ref, src_ref, live_ref, table_hbm,
    a_ref, b_ref, c_ref, white_ref,
    raw_v, tap_v, dec_v, sel_v, pair_v, trace_v, table_v, own_v, slot_v, place_v, block_v,
    load_sem, table_sem, halo_sem, pair_sem, trace_send, trace_recv,
    a_send, a_recv, b_send, b_recv, c_send, c_recv, own_sem, twin_send, twin_recv, spread_send, spread_recv,
):
    tm = lax.axis_index("tm")
    chan = lax.axis_index("chan")
    y, z_hi = tm // 4, lax.rem(tm, 4)
    z_lo, x, core = chan // 8, lax.rem(chan, 8) // 2, lax.rem(chan, 2)
    z = z_hi * 2 + z_lo
    direction = 1 - 2 * core
    half = lax.rem(tm, 2)

    def remote(src, dst, sems, device):
        return pltpu.make_async_remote_copy(
            src_ref=src, dst_ref=dst, send_sem=sems[0], recv_sem=sems[1], device_id=device, device_id_type=MESH
        )

    loads = []
    for part in range(4):
        loads.append(
            pltpu.make_async_copy(
                raw_hbm.at[:, part * 1280 : (part + 1) * 1280],
                raw_v.at[:, 128 + part * 1280 : 128 + (part + 1) * 1280],
                load_sem.at[part],
            )
        )
        loads[-1].start()
    table_load = pltpu.make_async_copy(table_hbm, table_v, table_sem)
    table_load.start()

    barrier = pltpu.get_barrier_semaphore()
    peers = [(lax.rem(tm + step, TM), chan) for step in range(1, TM)]
    twin = place(x, y, z, 1 - core)
    run = lax.rem(z, 4)
    spread = []
    for step in range(1, 32):
        to_run = lax.rem(run + step // 8, 4)
        to_x = lax.rem(x + step // 2, NX)
        to_core = lax.rem(core + step, NC)
        spread.append((place(to_x, y, z - run + to_run, to_core), to_run * 2 + to_core))
        peers.append(spread[-1][0])
    for step in (1, 3, 5, 7):
        peers.append(place(x, y, lax.rem(z + step, NZ), core))
    for peer in peers:
        pl.semaphore_signal(barrier, inc=1, device_id=peer, device_id_type=MESH)
    pl.semaphore_wait(barrier, len(peers))

    halo = remote(
        raw_hbm.at[:, 4992:5120], raw_v.at[:, 0:128], (halo_sem.at[0], halo_sem.at[1]), (lax.rem(tm + 1, TM), chan)
    )
    halo.start()

    base = pltpu.roll(jnp.broadcast_to(rev_ref[...], (8, 384)), 0, 1, stride=DECIM, stride_axis=0)
    for group in range(8):
        rows = []
        for octet in (2 * group, 2 * group + 1):
            at, turn = divmod(octet * 8 * DECIM, 128)
            piece = pltpu.roll(base, turn, 1) if turn else base
            blocks = [jnp.zeros((8, 128), F32)] * (REACH // 128)
            for number in range(min(3, REACH // 128 - at)):
                blocks[at + number] = piece[:, number * 128 : (number + 1) * 128]
            rows.append(jnp.concatenate(blocks, axis=1))
        band = jnp.concatenate(rows, axis=0)
        band_hi = band.astype(BF16)
        tap_v[group * 16 : group * 16 + 16, :] = band_hi
        tap_v[128 + group * 16 : 128 + group * 16 + 16, :] = (band - band_hi.astype(F32)).astype(BF16)

    src = src_ref[...].astype(F32)
    src_col = jnp.transpose(jnp.broadcast_to(src, (SRC, SRC)))
    lane = lax.broadcasted_iota(jnp.int32, (SRC, SRC), 1)
    row = lax.broadcasted_iota(jnp.int32, (SRC, SRC), 0)
    hit = jnp.where(src_col == (lane + chan * 256).astype(F32), 1.0, 0.0)
    is_src = jnp.sum(hit, axis=0, keepdims=True)
    earlier = jnp.where((row // 16 == lane // 16) & (row < lane), 1.0, 0.0)
    rank = dot(jnp.broadcast_to(is_src, (16, SRC)).astype(BF16), earlier.astype(BF16))[0:1, :]
    pick_row = lax.broadcasted_iota(jnp.int32, (32, SRC), 0)
    pick_lane = lax.broadcasted_iota(jnp.int32, (32, SRC), 1)
    pick = jnp.where(
        (pick_row // 2 == pick_lane // 16) & (lax.rem(pick_row, 2).astype(F32) == rank) & (is_src > 0.5), 1.0, 0.0
    ).astype(BF16)

    src_row = jnp.broadcast_to(src, (SRC, SRC))
    row_block = jnp.floor(src_row * (1.0 / 16))
    col_block = jnp.floor(src_col * (1.0 / 16))
    before = jnp.where((row_block == col_block) & (src_row < src_col), 1.0, 0.0)
    behind = jnp.sum(before, axis=1, keepdims=True).astype(jnp.int32)
    block_of = col_block[:, 0:1].astype(jnp.int32)
    chan_of, local_of = block_of // 16, lax.rem(block_of, 16)
    spot = ((local_of // 8) * 2 + chan_of // 8) * 128 + lax.rem(chan_of, 8) * 16 + 2 * lax.rem(local_of, 8) + behind
    place_v[...] = jnp.broadcast_to(spot, (SRC, 128))

    for part in (1, 2, 3, 0):
        if part == 1:
            loads[0].wait()
        if part:
            loads[part].wait()
        else:
            halo.wait()

            @pl.when(tm == 0)
            def _():
                raw_v[:, 0:128] = jnp.zeros((256, 128), BF16)

        both = lax.dot_general(
            raw_v[:, part * 1280 : part * 1280 + REACH],
            tap_v[...],
            (((1,), (1,)), ((), ())),
            preferred_element_type=F32,
        )
        dec_v[:, part * 128 : (part + 1) * 128] = (both[:, 0:128] + both[:, 128:256]).astype(BF16)

    picked = dot(pick, dec_v[...]).astype(BF16)
    sel_v[0] = picked[0:16]
    sel_v[1] = picked[16:32]
    pair = remote(
        sel_v.at[1 - half], pair_v, (pair_sem.at[0], pair_sem.at[1]), (tm + 1 - 2 * half, chan)
    )
    pair.start()

    pair.wait()
    traces = []
    for step in range(1, TM):
        to = lax.rem(tm + step, TM)
        copy = remote(
            dec_v.at[pl.ds(pl.multiple_of(to * 16, 16), 16), :],
            trace_v.at[tm],
            (trace_send.at[step - 1], trace_recv.at[step - 1]),
            (to, chan),
        )
        copy.start()
        traces.append(copy)
    trace_v[tm] = dec_v[pl.ds(pl.multiple_of(tm * 16, 16), 16), :]

    table_load.wait()
    spec = dot(jnp.concatenate([sel_v[half], pair_v[...]], axis=0), table_v[...])
    mine = spec[0:16, 0:SEG] + spec[0:16, SEG:]
    other = spec[16:32, 0:SEG] + spec[16:32, SEG:]
    is_first = half == 0
    sign = odd_sign(16)
    full = whiten(
        jnp.where(is_first, mine, other) + sign * jnp.where(is_first, other, mine), 32 * lax.rem(tm // 2, 4)
    )
    for band in range(KG):
        own_v[band] = full[:, band * 128 : (band + 1) * 128]

    here = run * 8 + x * 2 + core
    spreads = []
    for number, (peer, band) in enumerate(spread):
        copy = remote(own_v.at[band], slot_v.at[here], (spread_send.at[number], spread_recv.at[number]), peer)
        copy.start()
        spreads.append(copy)
    slot_v[here] = own_v[run * 2 + core]
    wanted = place_v[pl.ds(pl.multiple_of(x * QUOTA, QUOTA), QUOTA), :]
    slot_lane = lax.broadcasted_iota(jnp.int32, (QUOTA, 128), 1)
    chosen = jnp.concatenate(
        [jnp.where(wanted == slot_lane + part * 128, 1.0, 0.0) for part in range(SLOTS // 128)], axis=1
    ).astype(BF16)
    for copy in spreads:
        copy.wait()
    block_v[...] = dot(chosen, slot_v[...].reshape(SLOTS, 128)).astype(BF16)

    def part_order(buf, axes):
        sizes = {"x": NX, "y": NY, "z": NZ}
        at = {"x": x, "y": y, "z": z}
        order = []
        for number, axis in enumerate(axes):
            lead = [at[a] for a in reversed(axes[number + 1 :])]

            def chunk(index, lead=lead):
                return buf.at[(core, *lead, index)]

            def device(index, axis=axis):
                where = dict(at)
                where[axis] = index
                return place(where["x"], where["y"], where["z"], core)

            order.append((at[axis], sizes[axis], chunk, device))
        return order

    sends = []
    routines = []
    own_copies = []
    bufs = ((a_ref, "xyz", a_send, a_recv), (b_ref, "yzx", b_send, b_recv), (c_ref, "zxy", c_send, c_recv))
    for number, (buf, axes, send_sem, recv_sem) in enumerate(bufs):
        begin, rows = PARTS[number]
        first = block_v.at[begin : begin + rows]
        at = {"x": x, "y": y, "z": z}
        slot = buf.at[(core, *(at[a] for a in reversed(axes)))]
        copy = pltpu.make_async_copy(first, slot, own_sem.at[number])
        copy.start()
        own_copies.append(copy)
        order = part_order(buf, axes)
        routines.append(gather_part((send_sem, recv_sem), order, direction, sends, first))

    twins = []

    def to_twin(block):
        number = len(twins)
        copy = remote(block, block, (twin_send.at[number], twin_recv.at[number]), twin)
        copy.start()
        twins.append(copy)

    def advance(name):
        for block in routines["ABC".index(name)]:
            if block is None:
                break
            to_twin(block)

    def own_channels(part):
        rows = lax.broadcasted_iota(jnp.int32, (128, HALF), 0)
        alive = lax.rem(rows, 16) < live_ref[0]
        flat = trace_v[part * 8 : part * 8 + 8].reshape(128, HALF)
        spec = dot(jnp.where(alive, flat, jnp.zeros_like(flat)), table_v[...])
        for seg in range(NSEG // 2):
            low = spec[seg * 32 : seg * 32 + 16]
            high = spec[seg * 32 + 16 : seg * 32 + 32]
            full = low[:, 0:SEG] + low[:, SEG:] + sign * (high[:, 0:SEG] + high[:, SEG:])
            white = whiten(full).astype(F32)
            for band in range(KG):
                rows_at = pl.ds(part * 4 + seg, 16, stride=NSEG)
                white_ref[band, rows_at, :] = white[:, band * 128 : (band + 1) * 128]

    for name in "ABC":
        advance(name)
    for copy in own_copies:
        copy.wait()
    for copy in traces:
        copy.wait()
    own_channels(0)
    for number, name in enumerate(ROUNDS):
        if number == 4:
            own_channels(1)
        advance(name)
    for copy in sends:
        copy.wait_send()
    for copy in twins:
        copy.wait()


def correlate_kernel(white_ref, a_ref, b_ref, c_ref, lag_ref, out_hbm, all_v, weight_v, cross_v, out_v, out_sem):
    quarter = lax.broadcasted_iota(jnp.int32, (SRC, 128), 1) // 32
    quarter_b = quarter.astype(F32).astype(BF16)

    def merge(blocks, shift):
        full = blocks[(0 - shift) % 4]
        lanes = (quarter_b if full.dtype == BF16 else quarter)[0 : full.shape[0]]
        for j in range(1, 4):
            full = jnp.where(lanes == j, blocks[(j - shift) % 4], full)
        return full

    for band in range(KG):
        run, core = band // 2, band % 2
        for four in range(2):
            blocks = []
            for seg in range(four * 4, four * 4 + 4):
                y, z = seg // 2, (seg % 2) * 4 + run
                pieces = []
                for x in range(NX):
                    pieces += [a_ref[core, z, y, x], b_ref[core, x, z, y], c_ref[core, y, x, z]]
                blocks.append(jnp.concatenate(pieces, axis=0))
            for part in range(QUARTERS):
                lane = ((band * QUARTERS + part) * 2 + four) * 128
                all_v[:, lane : lane + 128] = merge(blocks, part)

    row = lax.broadcasted_iota(jnp.int32, (BINS, 128), 0)
    lane = lax.broadcasted_iota(jnp.int32, (BINS, 128), 1)
    same = row.astype(F32).astype(BF16) == lax.rem(lane, BINS).astype(F32).astype(BF16)

    def spread(rows, seg):
        wide = jnp.broadcast_to(rows[seg : seg + 1], (BINS, 128)).astype(BF16)
        return jnp.where(same, wide, jnp.zeros_like(wide))

    is_re = lax.rem(lane[0:8], 2 * BINS) < BINS

    def copies(which):
        return [
            pltpu.make_async_copy(
                out_v.at[which, part].reshape(SRC, 8, 128),
                out_hbm.at[:, which * 8 : which * 8 + 8, part * 128 : (part + 1) * 128],
                out_sem.at[which, part],
            )
            for part in range(3)
        ]

    @pl.loop(0, 2)
    def _(octet):
        @pl.loop(0, 4)
        def _(band_pair):
          for sub in range(2):
            band = band_pair * 2 + sub
            crosses = []
            turned = [pltpu.roll(white_ref[band, 8 * octet + c], 32 * (c % 4), 1) if c % 4 else white_ref[band, 8 * octet + c] for c in range(8)]
            for part in range(QUARTERS):
                slot = part % 2
                for group in range(2):
                    v = merge(turned[group * 4 : group * 4 + 4], part)
                    u = jnp.where(is_re, pltpu.roll(v, 128 - BINS, 1), -pltpu.roll(v, BINS, 1))
                    lanes = slice(group * 128, group * 128 + 128)
                    for four in range(2):
                        for j in range(4):
                            seg = four * 4 + (j - part) % 4
                            at = four * 128 + j * 32
                            weight_v[slot, at : at + 16, lanes] = spread(v, seg)
                            weight_v[slot, at + 16 : at + 32, lanes] = spread(u, seg)
                at = pl.multiple_of((band * QUARTERS + part) * 256, 256)
                crosses.append(dot(all_v[:, pl.ds(at, 256)], weight_v[slot]).astype(BF16))
            for c in range(8):
                blocks = [cross[:, c // 4 * 128 : c // 4 * 128 + 128] for cross in crosses]
                full = blocks[0]
                for part in range(1, 4):
                    full = jnp.where(quarter_b == (c + part) % 4, blocks[part], full)
                cross_v[c, :, pl.ds(pl.multiple_of(band * 128, 128), 128)] = full
        @pl.loop(0, 2)
        def _(four):
            for c in range(4):
                table = jnp.concatenate(
                    [
                        lag_ref[band * 128 + (j - c) % 4 * 32 : band * 128 + (j - c) % 4 * 32 + 32, :]
                        for band in range(KG)
                        for j in range(4)
                    ],
                    axis=0,
                )
                lags = dot(cross_v[four * 4 + c], table)
                for part in range(3):
                    out_v[octet, part, pl.ds(four * 4 + c, SRC, stride=8), :] = lags[:, part * 128 : (part + 1) * 128]

        for which in range(2):

            @pl.when(octet == which)
            def _():
                for copy in copies(which):
                    copy.start()

    for which in range(2):
        for copy in copies(which):
            copy.wait()


def local(raw_strain, fir_taps, source_channels, live_counts):
    rev = jnp.pad(jnp.flip(fir_taps), (1, 384 - 1 - TAPS))[None, :]
    src = source_channels[None, :]
    any_spec = pl.BlockSpec(memory_space=pl.ANY)
    vmem = pl.BlockSpec(memory_space=pltpu.VMEM)
    dma = pltpu.SemaphoreType.DMA
    heights = [rows for _, rows in PARTS]
    hops = NX - 1 + NY - 1 + NZ - 1
    blocks = NX + NY + NZ
    a, b, c, white = pl.pallas_call(
        gather_kernel,
        out_shape=(
            jax.ShapeDtypeStruct((NC, NZ, NY, NX, heights[0], 128), BF16),
            jax.ShapeDtypeStruct((NC, NX, NZ, NY, heights[1], 128), BF16),
            jax.ShapeDtypeStruct((NC, NY, NX, NZ, heights[2], 128), BF16),
            jax.ShapeDtypeStruct((KG, 16 * NSEG, 128), F32),
        ),
        in_specs=[any_spec, vmem, vmem, pl.BlockSpec(memory_space=pltpu.SMEM), any_spec],
        out_specs=(vmem, vmem, vmem, vmem),
        scratch_shapes=[
            pltpu.VMEM((256, 5248), BF16),
            pltpu.VMEM((256, REACH), BF16),
            pltpu.VMEM((256, HALF), BF16),
            pltpu.VMEM((2, 16, HALF), BF16),
            pltpu.VMEM((16, HALF), BF16),
            pltpu.VMEM((TM, 16, HALF), BF16),
            pltpu.VMEM((HALF, 2 * SEG), BF16),
            pltpu.VMEM((KG, 16, 128), BF16),
            pltpu.VMEM((32, 16, 128), BF16),
            pltpu.VMEM((SRC, 128), jnp.int32),
            pltpu.VMEM((QUOTA, 128), BF16),
            dma((4,)),
            dma,
            dma((2,)),
            dma((2,)),
            dma((TM - 1,)),
            dma((TM - 1,)),
            dma((hops,)),
            dma((hops,)),
            dma((hops,)),
            dma((hops,)),
            dma((hops,)),
            dma((hops,)),
            dma((3,)),
            dma((blocks,)),
            dma((blocks,)),
            dma((31,)),
            dma((31,)),
        ],
        compiler_params=pltpu.CompilerParams(
            collective_id=0, has_side_effects=True, vmem_limit_bytes=60 * 1024 * 1024
        ),
        name="filter_and_gather",
    )(raw_strain, rev, src, live_counts, jnp.asarray(dft_table()))
    return pl.pallas_call(
        correlate_kernel,
        out_shape=jax.ShapeDtypeStruct((SRC, 16, 2 * LAGH), F32),
        in_specs=[vmem, vmem, vmem, vmem, vmem],
        out_specs=any_spec,
        scratch_shapes=[
            pltpu.VMEM((SRC, NSEG * SEG), BF16),
            pltpu.VMEM((2, 256, 256), BF16),
            pltpu.VMEM((8, SRC, SEG), BF16),
            pltpu.VMEM((2, 3, SRC * 8, 128), F32),
            dma((2, 3)),
        ],
        compiler_params=pltpu.CompilerParams(vmem_limit_bytes=60 * 1024 * 1024),
        name="correlate",
    )(white.reshape(KG, 16, NSEG, 128), a, b, c, jnp.asarray(lag_table()))


def solution(mesh):
    placed = (P("chan", "tm"), P(), P(), P(("chan", "tm")))
    return jax.shard_map(
        local, mesh=mesh, in_specs=placed, out_specs=P(None, ("chan", "tm"), None), check_vma=False
    )
```

time: 97.6 us -> 82.4 us (0.84); the launches traced: 96.3 us -> 82.3 us
  Pallas kernels: 94.3 us -> 80.3 us
    pallas_call x1, Pallas kernels: 25.7 us -> 18 us  [local(): pl.pallas_call(correlate_kernel, out_shape=jax.ShapeDtypeStruct((SRC, 16,...]
    pallas_call x1, Pallas kernels: 68.6 us -> 62.3 us  [local(): pl.pallas_call(gather_kernel, out_shape=(jax.ShapeDtypeStruct((NC, NZ, NY...]
where the time goes in v1:
time: 82.4 us; the launch traced here: 82.3 us
  Pallas kernels  80.3 us (97%)
  local copies, waits for them, and re-layouts  1.39 us (2%)
    pallas_call x1, Pallas kernels, local(): pl.pallas_call(gather_kernel, out_shape=(jax.ShapeDtypeStruct((NC, NZ, NY...  62.3 us
    pallas_call x1, Pallas kernels, local(): pl.pallas_call(correlate_kernel, out_shape=jax.ShapeDtypeStruct((SRC, 16,...  18 us

profile of v1, /device:TPU:1, one launch (start us, length us, event | category | flops | bytes accessed | tf_op | source)
XLA Modules:
  0.0 82.3 jit_solution(10500115471061524523)
XLA Ops:
  0.7 0.7 rev.4
  1.4 0.1 pad.4
  1.5 0.6 broadcast_in_dim.6.rev_ref
  2.0 62.3 %filter_and_gather.1 = (bf16[2,8,4,4,16,128]{5,4,3,2,1,0:T(8,128)(2,1)}, bf16[2,4,8,4,16,128]{5,4,3,2,1,0:T(8,128)(2,1)}, bf16[2,4,4,8,32,128]{5,4,3,2,1,0:T(8,128)(2,1)}, f32[8,128,128]{2,1,0:T(8,128)}) custom-call(bf16[256,5120]{1,0:T(8,128)(2,1)} %raw_hbm.1, f32[1,384]{1,0:T(1,128)} %broadcast_in_dim.6.rev_ref, s32[1,256]{1,0:T(1,128)} %bitcast.3, ...), custom_call_target="tpu_custom_call" | custom-call | tf_op jit(solution)/shard_map/filter_and_gather/pallas_call | solution.py:485
  64.3 18.0 %correlate.1 = f32[256,16,384]{2,1,0:T(8,128)} custom-call(f32[8,16,8,128]{3,2,1,0:T(8,128)} %bitcast.2, bf16[2,8,4,4,16,128]{5,4,3,2,1,0:T(8,128)(2,1)} %get-tuple-element.10.a_ref, bf16[2,4,8,4,16,128]{5,4,3,2,1,0:T(8,128)(2,1)} %get-tuple-element.11.b_ref, bf16[2,4,4,8,32,128]{5,4,3,2,1,0:T(8,128)(2,1)} %get-tuple-element.12.c_ref, ...), custom_call_target="tpu_custom_call" | custom-call | tf_op jit(solution)/shard_map/correlate/pallas_call | solution.py:530

commit v2 on v1

--- a/solution.py
+++ b/solution.py
@@ -22,6 +22,7 @@
 TAPS = 128
 REACH = 1408
 KG = HALF // BAND
+EDGE = 16
 QUARTERS, BINS = 4, 16
 QUOTA = SRC // NX
 PARTS = ((0, 16), (16, 16), (32, 32))
@@ -132,9 +133,9 @@
 
 
 def gather_kernel(
-    raw_hbm, rev_ref, src_ref, live_ref, table_hbm,
+    raw_hbm, taps_ref, src_ref, live_ref, table_hbm,
     a_ref, b_ref, c_ref, white_ref,
-    raw_v, tap_v, dec_v, sel_v, pair_v, trace_v, table_v, own_v, slot_v, place_v, block_v,
+    raw_v, tap_v, dec_v, sel_v, pair_v, edge_v, trace_v, table_v, own_v, slot_v, place_v, block_v,
     load_sem, table_sem, halo_sem, pair_sem, trace_send, trace_recv,
     a_send, a_recv, b_send, b_recv, c_send, c_recv, own_sem, twin_send, twin_recv, spread_send, spread_recv,
 ):
@@ -179,14 +180,12 @@
         peers.append(place(x, y, lax.rem(z + step, NZ), core))
     for peer in peers:
         pl.semaphore_signal(barrier, inc=1, device_id=peer, device_id_type=MESH)
-    pl.semaphore_wait(barrier, len(peers))
-
-    halo = remote(
-        raw_hbm.at[:, 4992:5120], raw_v.at[:, 0:128], (halo_sem.at[0], halo_sem.at[1]), (lax.rem(tm + 1, TM), chan)
-    )
-    halo.start()
-
-    base = pltpu.roll(jnp.broadcast_to(rev_ref[...], (8, 384)), 0, 1, stride=DECIM, stride_axis=0)
+    taps_col = jnp.transpose(jnp.broadcast_to(taps_ref[...], (TAPS, TAPS)))
+    tap_row = lax.broadcasted_iota(jnp.int32, (TAPS, 384), 0)
+    tap_lane = lax.broadcasted_iota(jnp.int32, (TAPS, 384), 1)
+    taps_wide = jnp.concatenate([taps_col] * 3, axis=1)
+    rev = jnp.sum(jnp.where(tap_row + tap_lane == TAPS, taps_wide, 0.0), axis=0, keepdims=True)
+    base = pltpu.roll(jnp.broadcast_to(rev, (8, 384)), 0, 1, stride=DECIM, stride_axis=0)
     for group in range(8):
         rows = []
         for octet in (2 * group, 2 * group + 1):
@@ -225,35 +224,60 @@
     spot = ((local_of // 8) * 2 + chan_of // 8) * 128 + lax.rem(chan_of, 8) * 16 + 2 * lax.rem(local_of, 8) + behind
     place_v[...] = jnp.broadcast_to(spot, (SRC, 128))
 
-    for part in (1, 2, 3, 0):
-        if part == 1:
-            loads[0].wait()
-        if part:
-            loads[part].wait()
-        else:
-            halo.wait()
-
-            @pl.when(tm == 0)
-            def _():
-                raw_v[:, 0:128] = jnp.zeros((256, 128), BF16)
-
-        both = lax.dot_general(
-            raw_v[:, part * 1280 : part * 1280 + REACH],
-            tap_v[...],
-            (((1,), (1,)), ((), ())),
-            preferred_element_type=F32,
-        )
-        dec_v[:, part * 128 : (part + 1) * 128] = (both[:, 0:128] + both[:, 128:256]).astype(BF16)
+    def filtered(samples, taps):
+        both = lax.dot_general(samples, taps, (((1,), (1,)), ((), ())), preferred_element_type=F32)
+        return both[:, 0:128] + both[:, 128:256]
+
+    raw_v[:, 0:128] = jnp.zeros((256, 128), BF16)
+    heads = None
+    for part in range(4):
+        loads[part].wait()
+        sums = filtered(raw_v[:, part * 1280 : part * 1280 + REACH], tap_v[...])
+        dec_v[:, part * 128 : (part + 1) * 128] = sums.astype(BF16)
+        heads = sums if part == 0 else heads
+    tails = filtered(raw_v[:, 5120:5248], tap_v[:, 0:128])
+    edge_lane = lax.broadcasted_iota(jnp.int32, (256, 128), 1)
+    edge = jnp.where(edge_lane < 64, heads, pltpu.roll(tails, 64, 1))
+    edge = jnp.where(lax.rem(edge_lane, 64) < EDGE, edge, 0.0)
+    packed = jnp.zeros((256, 128), F32)
+    for number in range(3):
+        piece = edge.astype(BF16).astype(F32)
+        edge = edge - piece
+        packed = packed + (pltpu.roll(piece, number * EDGE, 1) if number else piece)
+    dec_v[:, HALF:] = packed.astype(BF16)
+
+    def joined(main, edges, before):
+        def whole(rows, at):
+            full = pltpu.roll(rows, 128 - at, 1) if at else rows
+            for number in (1, 2):
+                full = full + pltpu.roll(rows, 128 - at - number * EDGE, 1)
+            return full
+
+        sums = (whole(edges.astype(F32), 0) + whole(before.astype(F32), 64)).astype(BF16)
+        lanes = lax.broadcasted_iota(jnp.int32, sums.shape, 1)
+        first = jnp.where(lanes < EDGE, sums.astype(F32), main[:, 0:128].astype(F32)).astype(BF16)
+        return jnp.concatenate([first, main[:, 128:]], axis=1)
 
     picked = dot(pick, dec_v[...]).astype(BF16)
     sel_v[0] = picked[0:16]
     sel_v[1] = picked[16:32]
-    pair = remote(
-        sel_v.at[1 - half], pair_v, (pair_sem.at[0], pair_sem.at[1]), (tm + 1 - 2 * half, chan)
-    )
+    pl.semaphore_wait(barrier, len(peers))
+    pair = remote(sel_v.at[1 - half], pair_v, (pair_sem.at[0], pair_sem.at[1]), (tm + 1 - 2 * half, chan))
     pair.start()
+    edge_copies = []
+    for step in (1, 2):
+        copy = remote(
+            sel_v.at[(1 - half) if step == 1 else half, :, HALF:],
+            edge_v.at[step - 1],
+            (halo_sem.at[0, step - 1], halo_sem.at[1, step - 1]),
+            (lax.rem(tm + step, TM), chan),
+        )
+        copy.start()
+        edge_copies.append(copy)
 
     pair.wait()
+    for copy in edge_copies:
+        copy.wait()
     traces = []
     for step in range(1, TM):
         to = lax.rem(tm + step, TM)
@@ -268,13 +292,19 @@
     trace_v[tm] = dec_v[pl.ds(pl.multiple_of(tm * 16, 16), 16), :]
 
     table_load.wait()
-    spec = dot(jnp.concatenate([sel_v[half], pair_v[...]], axis=0), table_v[...])
-    mine = spec[0:16, 0:SEG] + spec[0:16, SEG:]
-    other = spec[16:32, 0:SEG] + spec[16:32, SEG:]
     is_first = half == 0
+    mine, other = sel_v[half].astype(F32), pair_v[...].astype(F32)
+    low, high = jnp.where(is_first, mine, other), jnp.where(is_first, other, mine)
+    tail = jnp.where(is_first, edge_v[0].astype(F32), edge_v[1].astype(F32))
+    tail = jnp.where(tm // 2 == 0, 0.0, tail)
+    low_edge, high_edge = low[:, HALF:], high[:, HALF:]
+    low = joined(low[:, 0:HALF].astype(BF16), low_edge, tail)
+    high = joined(high[:, 0:HALF].astype(BF16), high_edge, low_edge)
+    spec = dot(jnp.concatenate([low, high], axis=0), table_v[...])
     sign = odd_sign(16)
     full = whiten(
-        jnp.where(is_first, mine, other) + sign * jnp.where(is_first, other, mine), 32 * lax.rem(tm // 2, 4)
+        spec[0:16, 0:SEG] + spec[0:16, SEG:] + sign * (spec[16:32, 0:SEG] + spec[16:32, SEG:]),
+        32 * lax.rem(tm // 2, 4),
     )
     for band in range(KG):
         own_v[band] = full[:, band * 128 : (band + 1) * 128]
@@ -345,7 +375,13 @@
     def own_channels(part):
         rows = lax.broadcasted_iota(jnp.int32, (128, HALF), 0)
         alive = lax.rem(rows, 16) < live_ref[0]
-        flat = trace_v[part * 8 : part * 8 + 8].reshape(128, HALF)
+        main = trace_v[part * 8 : part * 8 + 8, :, 0:HALF].reshape(128, HALF)
+        edges = trace_v[part * 8 : part * 8 + 8, :, HALF:].reshape(128, 128).astype(F32)
+        if part:
+            before = trace_v[part * 8 - 1, :, HALF:].astype(F32)
+        else:
+            before = jnp.zeros((16, 128), F32)
+        flat = joined(main, edges, jnp.concatenate([before, edges[0:112]], axis=0))
         spec = dot(jnp.where(alive, flat, jnp.zeros_like(flat)), table_v[...])
         for seg in range(NSEG // 2):
             low = spec[seg * 32 : seg * 32 + 16]
@@ -377,12 +413,16 @@
     quarter = lax.broadcasted_iota(jnp.int32, (SRC, 128), 1) // 32
     quarter_b = quarter.astype(F32).astype(BF16)
 
-    def merge(blocks, shift):
-        full = blocks[(0 - shift) % 4]
-        lanes = (quarter_b if full.dtype == BF16 else quarter)[0 : full.shape[0]]
-        for j in range(1, 4):
-            full = jnp.where(lanes == j, blocks[(j - shift) % 4], full)
-        return full
+    def merge(blocks, shift, rows=16):
+        lanes = (quarter_b if blocks[0].dtype == BF16 else quarter)[0:rows]
+        masks = [lanes == j for j in range(4)]
+        pieces = []
+        for at in range(0, blocks[0].shape[0], rows):
+            full = blocks[(0 - shift) % 4][at : at + rows]
+            for j in range(1, 4):
+                full = jnp.where(masks[j], blocks[(j - shift) % 4][at : at + rows], full)
+            pieces.append(full)
+        return jnp.concatenate(pieces, axis=0) if len(pieces) > 1 else pieces[0]
 
     for band in range(KG):
         run, core = band // 2, band % 2
@@ -429,7 +469,7 @@
             for part in range(QUARTERS):
                 slot = part % 2
                 for group in range(2):
-                    v = merge(turned[group * 4 : group * 4 + 4], part)
+                    v = merge(turned[group * 4 : group * 4 + 4], part, 8)
                     u = jnp.where(is_re, pltpu.roll(v, 128 - BINS, 1), -pltpu.roll(v, BINS, 1))
                     lanes = slice(group * 128, group * 128 + 128)
                     for four in range(2):
@@ -442,9 +482,7 @@
                 crosses.append(dot(all_v[:, pl.ds(at, 256)], weight_v[slot]).astype(BF16))
             for c in range(8):
                 blocks = [cross[:, c // 4 * 128 : c // 4 * 128 + 128] for cross in crosses]
-                full = blocks[0]
-                for part in range(1, 4):
-                    full = jnp.where(quarter_b == (c + part) % 4, blocks[part], full)
+                full = merge(blocks, c)
                 cross_v[c, :, pl.ds(pl.multiple_of(band * 128, 128), 128)] = full
         @pl.loop(0, 2)
         def _(four):
@@ -474,10 +512,11 @@
 
 
 def local(raw_strain, fir_taps, source_channels, live_counts):
-    rev = jnp.pad(jnp.flip(fir_taps), (1, 384 - 1 - TAPS))[None, :]
+    taps = fir_taps[None, :]
     src = source_channels[None, :]
     any_spec = pl.BlockSpec(memory_space=pl.ANY)
     vmem = pl.BlockSpec(memory_space=pltpu.VMEM)
+    hbm = pl.BlockSpec(memory_space=pltpu.HBM)
     dma = pltpu.SemaphoreType.DMA
     heights = [rows for _, rows in PARTS]
     hops = NX - 1 + NY - 1 + NZ - 1
@@ -485,20 +524,21 @@
     a, b, c, white = pl.pallas_call(
         gather_kernel,
         out_shape=(
-            jax.ShapeDtypeStruct((NC, NZ, NY, NX, heights[0], 128), BF16),
-            jax.ShapeDtypeStruct((NC, NX, NZ, NY, heights[1], 128), BF16),
-            jax.ShapeDtypeStruct((NC, NY, NX, NZ, heights[2], 128), BF16),
-            jax.ShapeDtypeStruct((KG, 16 * NSEG, 128), F32),
+            pltpu.VMEM((NC, NZ, NY, NX, heights[0], 128), BF16),
+            pltpu.VMEM((NC, NX, NZ, NY, heights[1], 128), BF16),
+            pltpu.VMEM((NC, NY, NX, NZ, heights[2], 128), BF16),
+            pltpu.VMEM((KG, 16 * NSEG, 128), F32),
         ),
-        in_specs=[any_spec, vmem, vmem, pl.BlockSpec(memory_space=pltpu.SMEM), any_spec],
+        in_specs=[hbm, vmem, vmem, pl.BlockSpec(memory_space=pltpu.SMEM), hbm],
         out_specs=(vmem, vmem, vmem, vmem),
         scratch_shapes=[
             pltpu.VMEM((256, 5248), BF16),
             pltpu.VMEM((256, REACH), BF16),
-            pltpu.VMEM((256, HALF), BF16),
-            pltpu.VMEM((2, 16, HALF), BF16),
-            pltpu.VMEM((16, HALF), BF16),
-            pltpu.VMEM((TM, 16, HALF), BF16),
+            pltpu.VMEM((256, HALF + 128), BF16),
+            pltpu.VMEM((2, 16, HALF + 128), BF16),
+            pltpu.VMEM((16, HALF + 128), BF16),
+            pltpu.VMEM((2, 16, 128), BF16),
+            pltpu.VMEM((TM, 16, HALF + 128), BF16),
             pltpu.VMEM((HALF, 2 * SEG), BF16),
             pltpu.VMEM((KG, 16, 128), BF16),
             pltpu.VMEM((32, 16, 128), BF16),
@@ -506,7 +546,7 @@
             pltpu.VMEM((QUOTA, 128), BF16),
             dma((4,)),
             dma,
-            dma((2,)),
+            dma((2, 2)),
             dma((2,)),
             dma((TM - 1,)),
             dma((TM - 1,)),
@@ -523,10 +563,10 @@
             dma((31,)),
         ],
         compiler_params=pltpu.CompilerParams(
-            collective_id=0, has_side_effects=True, vmem_limit_bytes=60 * 1024 * 1024
+            collective_id=0, has_side_effects=True, vmem_limit_bytes=58 * 1024 * 1024
         ),
         name="filter_and_gather",
-    )(raw_strain, rev, src, live_counts, jnp.asarray(dft_table()))
+    )(raw_strain, taps, src, live_counts, jnp.asarray(dft_table()))
     return pl.pallas_call(
         correlate_kernel,
         out_shape=jax.ShapeDtypeStruct((SRC, 16, 2 * LAGH), F32),
@@ -539,7 +579,7 @@
             pltpu.VMEM((2, 3, SRC * 8, 128), F32),
             dma((2, 3)),
         ],
-        compiler_params=pltpu.CompilerParams(vmem_limit_bytes=60 * 1024 * 1024),
+        compiler_params=pltpu.CompilerParams(vmem_limit_bytes=36 * 1024 * 1024),
         name="correlate",
     )(white.reshape(KG, 16, NSEG, 128), a, b, c, jnp.asarray(lag_table()))
 

time: 82.4 us -> 73.1 us (0.89)
  Pallas kernels: 80.3 us -> 72.2 us
  local copies, waits for them, and re-layouts: 1.39 us -> 0.01 us
    pallas_call x1, Pallas kernels: 62.3 us -> 56.8 us  [local(): pl.pallas_call(gather_kernel, out_shape=(pltpu.VMEM((NC, NZ, NY, NX, heig...]
    pallas_call x1, Pallas kernels: 18 us -> 15.4 us  [local(): pl.pallas_call(correlate_kernel, out_shape=jax.ShapeDtypeStruct((SRC, 16,...]
where the time goes in v2:
time: 73.1 us; the launch traced here: 73 us
  Pallas kernels  72.2 us (99%)
  between operations  0.74 us (1%)
    pallas_call x1, Pallas kernels, local(): pl.pallas_call(gather_kernel, out_shape=(pltpu.VMEM((NC, NZ, NY, NX, heig...  56.8 us
    pallas_call x1, Pallas kernels, local(): pl.pallas_call(correlate_kernel, out_shape=jax.ShapeDtypeStruct((SRC, 16,...  15.4 us

profile of v2, /device:TPU:1, one launch (start us, length us, event | category | flops | bytes accessed | tf_op | source)
XLA Modules:
  0.0 73.0 jit_solution(17488834368290856987)
XLA Ops:
  0.0 0.0 copy-start
  0.7 56.8 %filter_and_gather.1 = (bf16[2,8,4,4,16,128]{5,4,3,2,1,0:T(8,128)(2,1)S(1)}, bf16[2,4,8,4,16,128]{5,4,3,2,1,0:T(8,128)(2,1)S(1)}, bf16[2,4,4,8,32,128]{5,4,3,2,1,0:T(8,128)(2,1)S(1)}, f32[8,128,128]{2,1,0:T(8,128)S(1)}) custom-call(bf16[256,5120]{1,0:T(8,128)(2,1)} %raw_hbm.1, f32[1,128]{1,0:T(1,128)} %bitcast.5, s32[1,256]{1,0:T(1,128)} %bitcast.4, ...), custom_call_target="tpu_custom_call" | custom-call | tf_op jit(solution)/shard_map/filter_and_gather/pallas_call | solution.py:524
  57.6 0.0 copy-done
  57.6 15.4 %correlate.1 = f32[256,16,384]{2,1,0:T(8,128)} custom-call(f32[8,16,8,128]{3,2,1,0:T(8,128)S(1)} %bitcast.3, bf16[2,8,4,4,16,128]{5,4,3,2,1,0:T(8,128)(2,1)S(1)} %get-tuple-element.10.a_ref, bf16[2,4,8,4,16,128]{5,4,3,2,1,0:T(8,128)(2,1)S(1)} %get-tuple-element.11.b_ref, bf16[2,4,4,8,32,128]{5,4,3,2,1,0:T(8,128)(2,1)S(1)} %get-tuple-element.12.c_ref, ...), custom_call_target="tpu_custom_call" | custom-call | tf_op jit(solution)/shard_map/correlate/pallas_call | solution.py:570
Async XLA Ops:
  0.0 57.6 %copy-start = (bf16[1024,384]{1,0:T(8,128)(2,1)S(1)}, bf16[1024,384]{1,0:T(8,128)(2,1)}, u32[]{:S(2)}) copy-start(bf16[1024,384]{1,0:T(8,128)(2,1)} %constant.5.clone.lag_ref) | copy-start | bytes 2359300

commit v3 on v2

--- a/solution.py
+++ b/solution.py
@@ -25,8 +25,9 @@
 EDGE = 16
 QUARTERS, BINS = 4, 16
 QUOTA = SRC // NX
-PARTS = ((0, 16), (16, 16), (32, 32))
-ROUNDS = "ABCABACABABCAC"
+PARTS = ((0, 16), (16, 16), (32, 16), (48, 16))
+ROUNDS = "ABCDACDBAACBADABCDABACBCADAD"
+CUTS = (2, 2, 2, 2)
 
 
 def dot(a, b):
@@ -77,7 +78,7 @@
     return (y * 4 + z // 2, lax.rem(z, 2) * 8 + x * 2 + core)
 
 
-def gather_part(semaphores, order, step_dir, sends, first):
+def gather_part(semaphores, order, step_dir, sends, first, cuts):
     send_sem, recv_sem = semaphores
     count = 0
     for stage, (me, size, chunk, device) in enumerate(order):
@@ -116,28 +117,46 @@
             count += size - 1
             continue
         far, near = size // 2, size - 1 - size // 2
-        send(own, own, 1, count)
-        send(own, own, -1, count + far)
-        yield own
+
+        def piece(index, cut):
+            block = chunk(index)
+            depth = block.shape[0] // cuts
+            return block.at[cut * depth : (cut + 1) * depth]
+
+        def arrived_piece(offset, number, cut):
+            block = piece(index(offset), cut)
+            copy_of((block, block), 1, number).wait_recv()
+            return block
+
+        def number_of(hop, cut):
+            return count + hop * cuts + cut
+
+        for cut in range(cuts):
+            own = piece(me, cut)
+            send(own, own, 1, number_of(0, cut))
+            send(own, own, -1, number_of(far, cut))
+        for cut in range(cuts):
+            yield piece(me, cut)
         for hop in range(1, far + 1):
-            yield None
-            block = arrived(-hop, count + hop - 1)
-            if hop < far:
-                send(block, block, 1, count + hop)
-            yield block
-            if hop <= near:
-                block = arrived(hop, count + far + hop - 1)
-                if hop < near:
-                    send(block, block, -1, count + far + hop)
+            for cut in range(cuts):
+                yield None
+                block = arrived_piece(-hop, number_of(hop - 1, cut), cut)
+                if hop < far:
+                    send(block, block, 1, number_of(hop, cut))
                 yield block
+                if hop <= near:
+                    block = arrived_piece(hop, number_of(far + hop - 1, cut), cut)
+                    if hop < near:
+                        send(block, block, -1, number_of(far + hop, cut))
+                    yield block
 
 
 def gather_kernel(
     raw_hbm, taps_ref, src_ref, live_ref, table_hbm,
-    a_ref, b_ref, c_ref, white_ref,
+    a_ref, b_ref, c_ref, d_ref, white_ref,
     raw_v, tap_v, dec_v, sel_v, pair_v, edge_v, trace_v, table_v, own_v, slot_v, place_v, block_v,
     load_sem, table_sem, halo_sem, pair_sem, trace_send, trace_recv,
-    a_send, a_recv, b_send, b_recv, c_send, c_recv, own_sem, twin_send, twin_recv, spread_send, spread_recv,
+    a_send, a_recv, b_send, b_recv, c_send, c_recv, d_send, d_recv, own_sem, twin_send, twin_recv, spread_send, spread_recv,
 ):
     tm = lax.axis_index("tm")
     chan = lax.axis_index("chan")
@@ -278,19 +297,6 @@
     pair.wait()
     for copy in edge_copies:
         copy.wait()
-    traces = []
-    for step in range(1, TM):
-        to = lax.rem(tm + step, TM)
-        copy = remote(
-            dec_v.at[pl.ds(pl.multiple_of(to * 16, 16), 16), :],
-            trace_v.at[tm],
-            (trace_send.at[step - 1], trace_recv.at[step - 1]),
-            (to, chan),
-        )
-        copy.start()
-        traces.append(copy)
-    trace_v[tm] = dec_v[pl.ds(pl.multiple_of(tm * 16, 16), 16), :]
-
     table_load.wait()
     is_first = half == 0
     mine, other = sel_v[half].astype(F32), pair_v[...].astype(F32)
@@ -316,6 +322,19 @@
         copy.start()
         spreads.append(copy)
     slot_v[here] = own_v[run * 2 + core]
+
+    traces = []
+    for step in range(1, TM):
+        to = lax.rem(tm + step, TM)
+        copy = remote(
+            dec_v.at[pl.ds(pl.multiple_of(to * 16, 16), 16), :],
+            trace_v.at[tm],
+            (trace_send.at[step - 1], trace_recv.at[step - 1]),
+            (to, chan),
+        )
+        copy.start()
+        traces.append(copy)
+    trace_v[tm] = dec_v[pl.ds(pl.multiple_of(tm * 16, 16), 16), :]
     wanted = place_v[pl.ds(pl.multiple_of(x * QUOTA, QUOTA), QUOTA), :]
     slot_lane = lax.broadcasted_iota(jnp.int32, (QUOTA, 128), 1)
     chosen = jnp.concatenate(
@@ -346,7 +365,12 @@
     sends = []
     routines = []
     own_copies = []
-    bufs = ((a_ref, "xyz", a_send, a_recv), (b_ref, "yzx", b_send, b_recv), (c_ref, "zxy", c_send, c_recv))
+    bufs = (
+        (a_ref, "xyz", a_send, a_recv),
+        (b_ref, "yzx", b_send, b_recv),
+        (c_ref, "zxy", c_send, c_recv),
+        (d_ref, "zxy", d_send, d_recv),
+    )
     for number, (buf, axes, send_sem, recv_sem) in enumerate(bufs):
         begin, rows = PARTS[number]
         first = block_v.at[begin : begin + rows]
@@ -356,7 +380,7 @@
         copy.start()
         own_copies.append(copy)
         order = part_order(buf, axes)
-        routines.append(gather_part((send_sem, recv_sem), order, direction, sends, first))
+        routines.append(gather_part((send_sem, recv_sem), order, direction, sends, first, CUTS[number]))
 
     twins = []
 
@@ -367,7 +391,7 @@
         twins.append(copy)
 
     def advance(name):
-        for block in routines["ABC".index(name)]:
+        for block in routines["ABCD".index(name)]:
             if block is None:
                 break
             to_twin(block)
@@ -392,7 +416,7 @@
                 rows_at = pl.ds(part * 4 + seg, 16, stride=NSEG)
                 white_ref[band, rows_at, :] = white[:, band * 128 : (band + 1) * 128]
 
-    for name in "ABC":
+    for name in "ABCD":
         advance(name)
     for copy in own_copies:
         copy.wait()
@@ -400,7 +424,7 @@
         copy.wait()
     own_channels(0)
     for number, name in enumerate(ROUNDS):
-        if number == 4:
+        if number == 5:
             own_channels(1)
         advance(name)
     for copy in sends:
@@ -409,7 +433,7 @@
         copy.wait()
 
 
-def correlate_kernel(white_ref, a_ref, b_ref, c_ref, lag_ref, out_hbm, all_v, weight_v, cross_v, out_v, out_sem):
+def correlate_kernel(white_ref, a_ref, b_ref, c_ref, d_ref, lag_ref, out_hbm, all_v, weight_v, cross_v, out_v, out_sem):
     quarter = lax.broadcasted_iota(jnp.int32, (SRC, 128), 1) // 32
     quarter_b = quarter.astype(F32).astype(BF16)
 
@@ -432,7 +456,7 @@
                 y, z = seg // 2, (seg % 2) * 4 + run
                 pieces = []
                 for x in range(NX):
-                    pieces += [a_ref[core, z, y, x], b_ref[core, x, z, y], c_ref[core, y, x, z]]
+                    pieces += [a_ref[core, z, y, x], b_ref[core, x, z, y], c_ref[core, y, x, z], d_ref[core, y, x, z]]
                 blocks.append(jnp.concatenate(pieces, axis=0))
             for part in range(QUARTERS):
                 lane = ((band * QUARTERS + part) * 2 + four) * 128
@@ -519,18 +543,21 @@
     hbm = pl.BlockSpec(memory_space=pltpu.HBM)
     dma = pltpu.SemaphoreType.DMA
     heights = [rows for _, rows in PARTS]
-    hops = NX - 1 + NY - 1 + NZ - 1
-    blocks = NX + NY + NZ
-    a, b, c, white = pl.pallas_call(
+    early = (NX + NY - 2, NY + NZ - 2, NZ + NX - 2, NZ + NX - 2)
+    last = (NZ, NX, NY, NY)
+    hops = [start + (size - 1) * cuts for start, size, cuts in zip(early, last, CUTS)]
+    blocks = sum(size * cuts for size, cuts in zip(last, CUTS))
+    a, b, c, d, white = pl.pallas_call(
         gather_kernel,
         out_shape=(
             pltpu.VMEM((NC, NZ, NY, NX, heights[0], 128), BF16),
             pltpu.VMEM((NC, NX, NZ, NY, heights[1], 128), BF16),
             pltpu.VMEM((NC, NY, NX, NZ, heights[2], 128), BF16),
+            pltpu.VMEM((NC, NY, NX, NZ, heights[3], 128), BF16),
             pltpu.VMEM((KG, 16 * NSEG, 128), F32),
         ),
         in_specs=[hbm, vmem, vmem, pl.BlockSpec(memory_space=pltpu.SMEM), hbm],
-        out_specs=(vmem, vmem, vmem, vmem),
+        out_specs=(vmem, vmem, vmem, vmem, vmem),
         scratch_shapes=[
             pltpu.VMEM((256, 5248), BF16),
             pltpu.VMEM((256, REACH), BF16),
@@ -550,13 +577,8 @@
             dma((2,)),
             dma((TM - 1,)),
             dma((TM - 1,)),
-            dma((hops,)),
-            dma((hops,)),
-            dma((hops,)),
-            dma((hops,)),
-            dma((hops,)),
-            dma((hops,)),
-            dma((3,)),
+            *(dma((count,)) for count in hops for _ in range(2)),
+            dma((4,)),
             dma((blocks,)),
             dma((blocks,)),
             dma((31,)),
@@ -570,7 +592,7 @@
     return pl.pallas_call(
         correlate_kernel,
         out_shape=jax.ShapeDtypeStruct((SRC, 16, 2 * LAGH), F32),
-        in_specs=[vmem, vmem, vmem, vmem, vmem],
+        in_specs=[vmem, vmem, vmem, vmem, vmem, vmem],
         out_specs=any_spec,
         scratch_shapes=[
             pltpu.VMEM((SRC, NSEG * SEG), BF16),
@@ -581,7 +603,7 @@
         ],
         compiler_params=pltpu.CompilerParams(vmem_limit_bytes=36 * 1024 * 1024),
         name="correlate",
-    )(white.reshape(KG, 16, NSEG, 128), a, b, c, jnp.asarray(lag_table()))
+    )(white.reshape(KG, 16, NSEG, 128), a, b, c, d, jnp.asarray(lag_table()))
 
 
 def solution(mesh):

time: 73.1 us -> 68.7 us (0.940)
  Pallas kernels: 72.2 us -> 67.9 us
    pallas_call x1, Pallas kernels: 56.8 us -> 52.5 us  [local(): pl.pallas_call(gather_kernel, out_shape=(pltpu.VMEM((NC, NZ, NY, NX, heig...]
where the time goes in v3:
time: 68.7 us; the launch traced here: 68.6 us
  Pallas kernels  67.9 us (99%)
  between operations  0.74 us (1%)
    pallas_call x1, Pallas kernels, local(): pl.pallas_call(gather_kernel, out_shape=(pltpu.VMEM((NC, NZ, NY, NX, heig...  52.5 us
    pallas_call x1, Pallas kernels, local(): pl.pallas_call(correlate_kernel, out_shape=jax.ShapeDtypeStruct((SRC, 16,...  15.4 us

profile of v3, /device:TPU:1, one launch (start us, length us, event | category | flops | bytes accessed | tf_op | source)
XLA Modules:
  0.0 68.6 jit_solution(8809633079006255420)
XLA Ops:
  0.0 0.0 copy-start
  0.7 52.5 %filter_and_gather.1 = (bf16[2,8,4,4,16,128]{5,4,3,2,1,0:T(8,128)(2,1)S(1)}, bf16[2,4,8,4,16,128]{5,4,3,2,1,0:T(8,128)(2,1)S(1)}, bf16[2,4,4,8,16,128]{5,4,3,2,1...) custom-call(bf16[256,5120]{1,0:T(8,128)(2,1)} %raw_hbm.1, f32[1,128]{1,0:T(1,128)} %bitcast.5, ...), custom_call_target="tpu_custom_call" | custom-call | tf_op jit(solution)/shard_map/filter_and_gather/pallas_call | solution.py:550
  53.2 0.0 copy-done
  53.2 15.4 %correlate.1 = f32[256,16,384]{2,1,0:T(8,128)} custom-call(f32[8,16,8,128]{3,2,1,0:T(8,128)S(1)} %bitcast.3, bf16[2,8,4,4,16,128]{5,4,3,2,1,0:T(8,128)(2,1)S(1)} %get-tuple-element.11.a_ref, bf16[2,4,8,4,16,128]{5,4,3,2,1,0:T(8,128)(2,1)S(1)} %get-tuple-element.12.b_ref, bf16[2,4,4,8,16,128]{5,4,3,2,1,0:T(8,128)(2,1)S(1)} %get-tuple-element.13.c_ref, ...), custom_call_target="tpu_custom_call" | custom-call | tf_op jit(solution)/shard_map/correlate/pallas_call | solution.py:592
Async XLA Ops:
  0.0 53.2 %copy-start = (bf16[1024,384]{1,0:T(8,128)(2,1)S(1)}, bf16[1024,384]{1,0:T(8,128)(2,1)}, u32[]{:S(2)}) copy-start(bf16[1024,384]{1,0:T(8,128)(2,1)} %constant.5.clone.lag_ref) | copy-start | bytes 2359300

commit v4 on v3

--- a/solution.py
+++ b/solution.py
@@ -484,14 +484,14 @@
 
     @pl.loop(0, 2)
     def _(octet):
-        @pl.loop(0, 4)
-        def _(band_pair):
-          for sub in range(2):
-            band = band_pair * 2 + sub
+        @pl.loop(0, 2)
+        def _(band_group):
+          for sub in range(4):
+            band = band_group * 4 + sub
             crosses = []
             turned = [pltpu.roll(white_ref[band, 8 * octet + c], 32 * (c % 4), 1) if c % 4 else white_ref[band, 8 * octet + c] for c in range(8)]
             for part in range(QUARTERS):
-                slot = part % 2
+                slot = (sub * QUARTERS + part) % 8
                 for group in range(2):
                     v = merge(turned[group * 4 : group * 4 + 4], part, 8)
                     u = jnp.where(is_re, pltpu.roll(v, 128 - BINS, 1), -pltpu.roll(v, BINS, 1))
@@ -596,7 +596,7 @@
         out_specs=any_spec,
         scratch_shapes=[
             pltpu.VMEM((SRC, NSEG * SEG), BF16),
-            pltpu.VMEM((2, 256, 256), BF16),
+            pltpu.VMEM((8, 256, 256), BF16),
             pltpu.VMEM((8, SRC, SEG), BF16),
             pltpu.VMEM((2, 3, SRC * 8, 128), F32),
             dma((2, 3)),

time: 68.7 us -> 67.8 us (0.987)
  Pallas kernels: 67.9 us -> 66.9 us
    pallas_call x1, Pallas kernels: 15.4 us -> 14.5 us  [local(): pl.pallas_call(correlate_kernel, out_shape=jax.ShapeDtypeStruct((SRC, 16,...]
where the time goes in v4:
time: 67.8 us; the launch traced here: 67.7 us
  Pallas kernels  66.9 us (99%)
  between operations  0.74 us (1%)
    pallas_call x1, Pallas kernels, local(): pl.pallas_call(gather_kernel, out_shape=(pltpu.VMEM((NC, NZ, NY, NX, heig...  52.5 us
    pallas_call x1, Pallas kernels, local(): pl.pallas_call(correlate_kernel, out_shape=jax.ShapeDtypeStruct((SRC, 16,...  14.5 us

profile of v4, /device:TPU:1, one launch (start us, length us, event | category | flops | bytes accessed | tf_op | source)
XLA Modules:
  0.0 67.7 jit_solution(219271158242336239)
XLA Ops:
  0.0 0.0 copy-start
  0.7 52.5 %filter_and_gather.1 = (bf16[2,8,4,4,16,128]{5,4,3,2,1,0:T(8,128)(2,1)S(1)}, bf16[2,4,8,4,16,128]{5,4,3,2,1,0:T(8,128)(2,1)S(1)}, bf16[2,4,4,8,16,128]{5,4,3,2,1...) custom-call(bf16[256,5120]{1,0:T(8,128)(2,1)} %raw_hbm.1, f32[1,128]{1,0:T(1,128)} %bitcast.5, ...), custom_call_target="tpu_custom_call" | custom-call | tf_op jit(solution)/shard_map/filter_and_gather/pallas_call | solution.py:550
  53.2 0.0 copy-done
  53.2 14.5 %correlate.1 = f32[256,16,384]{2,1,0:T(8,128)} custom-call(f32[8,16,8,128]{3,2,1,0:T(8,128)S(1)} %bitcast.3, bf16[2,8,4,4,16,128]{5,4,3,2,1,0:T(8,128)(2,1)S(1)} %get-tuple-element.11.a_ref, bf16[2,4,8,4,16,128]{5,4,3,2,1,0:T(8,128)(2,1)S(1)} %get-tuple-element.12.b_ref, bf16[2,4,4,8,16,128]{5,4,3,2,1,0:T(8,128)(2,1)S(1)} %get-tuple-element.13.c_ref, ...), custom_call_target="tpu_custom_call" | custom-call | tf_op jit(solution)/shard_map/correlate/pallas_call | solution.py:592
Async XLA Ops:
  0.0 53.2 %copy-start = (bf16[1024,384]{1,0:T(8,128)(2,1)S(1)}, bf16[1024,384]{1,0:T(8,128)(2,1)}, u32[]{:S(2)}) copy-start(bf16[1024,384]{1,0:T(8,128)(2,1)} %constant.5.clone.lag_ref) | copy-start | bytes 2359300

commit v5 on v4

--- a/solution.py
+++ b/solution.py
@@ -26,8 +26,8 @@
 QUARTERS, BINS = 4, 16
 QUOTA = SRC // NX
 PARTS = ((0, 16), (16, 16), (32, 16), (48, 16))
-ROUNDS = "ABCDACDBAACBADABCDABACBCADAD"
-CUTS = (2, 2, 2, 2)
+ROUNDS = "ABCDACDBAAAACBADAAABCDAAABACBCADAAAD"
+CUTS = (4, 2, 2, 2)
 
 
 def dot(a, b):

time: 67.8 us -> 68.3 us (level)
  no operation moved by 1% of the time
where the time goes in v5:
time: 68.3 us; the launch traced here: 68.2 us
  Pallas kernels  67.4 us (99%)
  between operations  0.74 us (1%)
    pallas_call x1, Pallas kernels, local(): pl.pallas_call(gather_kernel, out_shape=(pltpu.VMEM((NC, NZ, NY, NX, heig...  53 us
    pallas_call x1, Pallas kernels, local(): pl.pallas_call(correlate_kernel, out_shape=jax.ShapeDtypeStruct((SRC, 16,...  14.5 us

profile of v5, /device:TPU:1, one launch (start us, length us, event | category | flops | bytes accessed | tf_op | source)
XLA Modules:
  0.0 68.2 jit_solution(12185766176868966799)
XLA Ops:
  0.0 0.0 copy-start
  0.7 53.0 %filter_and_gather.1 = (bf16[2,8,4,4,16,128]{5,4,3,2,1,0:T(8,128)(2,1)S(1)}, bf16[2,4,8,4,16,128]{5,4,3,2,1,0:T(8,128)(2,1)S(1)}, bf16[2,4,4,8,16,128]{5,4,3,2,1...) custom-call(bf16[256,5120]{1,0:T(8,128)(2,1)} %raw_hbm.1, f32[1,128]{1,0:T(1,128)} %bitcast.5, ...), custom_call_target="tpu_custom_call" | custom-call | tf_op jit(solution)/shard_map/filter_and_gather/pallas_call | solution.py:550
  53.7 0.0 copy-done
  53.7 14.5 %correlate.1 = f32[256,16,384]{2,1,0:T(8,128)} custom-call(f32[8,16,8,128]{3,2,1,0:T(8,128)S(1)} %bitcast.3, bf16[2,8,4,4,16,128]{5,4,3,2,1,0:T(8,128)(2,1)S(1)} %get-tuple-element.11.a_ref, bf16[2,4,8,4,16,128]{5,4,3,2,1,0:T(8,128)(2,1)S(1)} %get-tuple-element.12.b_ref, bf16[2,4,4,8,16,128]{5,4,3,2,1,0:T(8,128)(2,1)S(1)} %get-tuple-element.13.c_ref, ...), custom_call_target="tpu_custom_call" | custom-call | tf_op jit(solution)/shard_map/correlate/pallas_call | solution.py:592
Async XLA Ops:
  0.0 53.7 %copy-start = (bf16[1024,384]{1,0:T(8,128)(2,1)S(1)}, bf16[1024,384]{1,0:T(8,128)(2,1)}, u32[]{:S(2)}) copy-start(bf16[1024,384]{1,0:T(8,128)(2,1)} %constant.5.clone.lag_ref) | copy-start | bytes 2359300
